TPU v7x, 256 devices: a whole 4x4x8 slice. The times are simulated.
256 devices in a mesh: seq: 8 (over y, core), item: 32 (over z, x).
Axes of the slice: x: 4, y: 4, z: 8, core: 2. Of those that a mesh axis runs over, the one named last changes fastest.
Arguments:
- events: float32 [32, 1024, 512], P('item', 'seq'), may hold values from -6 to 6
- w_uvqk: float32 [512, 2048], replicated, may hold values from -0.25 to 0.25
- out_gain: float32 [512], replicated, may hold values from 0.5 to 1.5
- w_out: float32 [512, 512], replicated, may hold values from -0.25 to 0.25
- item_table: float32 [32768, 512], P('item'), may hold values from -0.25 to 0.25
- user_lengths: int32 [32, 4], P('item'), may hold values from 1 to 512, 1024 in all within a row
- neg_ids: int32 [4, 512], replicated, may hold values from 0 to 1023
- panel_owner: int32 [4], replicated, may hold values from 0 to 31
- block_mask: int32 [32, 8], P('item', 'seq'), may hold values from 1 to 65535
- targets: int32 [32, 1024], P('item', 'seq'), may hold values from 0 to 2047
Outputs:
- mean_loss: float32 [], replicated
- event_grad: float32 [32, 1024, 512], P('item', 'seq')
- table_grad: float32 [32768, 512], P('item')
Inputs may be any that keep to these rules, and one draw needn't show every extreme that they name: `user_lengths`: the 4 lengths of a group sum to 1024, the longest is exactly 512. `neg_ids`: rows may repeat within and across panels. `panel_owner`: several panels may have one owner. `block_mask`: bit k of an entry admits negative columns 128 k to 128 k + 127 for the 128 events of that block.
All inputs are finite; a program needn't handle non-finite values.
Results may differ from a plain program's by a relative error of at most 0.0003.
Values sent between devices are 32-bit elements; how exact they have to be, the bound alone decides.
A program may use at most 64 MiB of HBM per device.

v0:
```python
import jax
import jax.numpy as jnp
from jax import lax
from jax.sharding import PartitionSpec as P

H = 16
highest = lax.Precision.HIGHEST
beta_weight = 0.75
epsilon = 1e-05


def broadcast(shard, axis, root):
    mine = lax.axis_index(axis) == root
    return lax.psum(jnp.where(mine, shard, jnp.zeros_like(shard)), axis)


def user_index(lengths, positions):
    user_ends = jnp.cumsum(lengths)
    return jnp.sum((positions[:, None] >= user_ends[None, :]).astype(jnp.int32), axis=1)


def pointwise(query_rows, key_rows, value_rows, query_pos, key_pos, query_user, key_user):
    scores = jnp.einsum("qhd,khd->hqk", query_rows, key_rows, precision=highest)
    allowed = (query_user[:, None] == key_user[None, :]) & (query_pos[:, None] >= key_pos[None, :])
    weights = jax.nn.silu(scores) * allowed[None, :, :].astype(jnp.float32)
    return jnp.einsum("hqk,khd->qhd", weights, value_rows, precision=highest)


def loss_terms(outputs, negatives, mask_words, target_cols):
    logits = jnp.einsum("td,nd->tn", outputs, negatives, precision=highest)
    columns = jnp.arange(negatives.shape[0], dtype=jnp.int32)
    mask_bits = jnp.repeat(mask_words, 128)
    live_cols = jnp.bitwise_and(
        jnp.right_shift(mask_bits[:, None], columns[None, :] // 128), 1
    ).astype(jnp.float32)
    is_target = (columns[None, :] == target_cols[:, None]).astype(jnp.float32)
    neg_weight = live_cols * (1.0 - is_target)
    loss_part = jnp.sum(
        beta_weight * is_target * jax.nn.softplus(-logits) + neg_weight * jax.nn.softplus(logits)
    )
    grad_logits = neg_weight * jax.nn.sigmoid(logits) - beta_weight * is_target * jax.nn.sigmoid(
        -logits
    )
    grad_rows = jnp.dot(grad_logits, negatives, precision=highest)
    panel_part = jnp.einsum("tn,td->nd", grad_logits, outputs, precision=highest)
    return (loss_part, grad_rows, panel_part)


def per_device(
    events,
    w_uvqk,
    out_gain,
    w_out,
    item_table,
    user_lengths,
    neg_ids,
    panel_owner,
    block_mask,
    targets,
):
    rows_in = events[0]
    tok_rows, width = rows_in.shape
    head_size = width // H
    lengths = user_lengths[0]
    projected = jax.nn.silu(jnp.dot(rows_in, w_uvqk, precision=highest))
    gates_u = projected[:, :width]
    packed = projected[:, width:].reshape(tok_rows, 3, H, head_size)
    spread = lax.all_to_all(packed, "seq", split_axis=2, concat_axis=0, tiled=True)
    group_len = spread.shape[0]
    positions = jnp.arange(group_len, dtype=jnp.int32)
    user_ids = user_index(lengths, positions)
    block_rows = 512

    def one_block(first_row):
        query_rows = lax.dynamic_slice_in_dim(spread[:, 1], first_row, block_rows, 0)
        query_pos = first_row + jnp.arange(block_rows, dtype=jnp.int32)
        query_user = lax.dynamic_slice_in_dim(user_ids, first_row, block_rows, 0)
        return pointwise(
            query_rows, spread[:, 2], spread[:, 0], query_pos, positions, query_user, user_ids
        )

    firsts = jnp.arange(group_len // block_rows, dtype=jnp.int32) * block_rows
    attended = lax.map(one_block, firsts).reshape(group_len, spread.shape[2], head_size)
    attended = lax.all_to_all(attended, "seq", split_axis=0, concat_axis=1, tiled=True)
    attended = attended.reshape(tok_rows, width)
    row_mean = jnp.mean(attended, axis=1, keepdims=True)
    centered = attended - row_mean
    variance = jnp.mean(centered * centered, axis=1, keepdims=True)
    normed = centered * lax.rsqrt(variance + epsilon) * out_gain
    outputs = rows_in + jnp.dot(normed * gates_u, w_out, precision=highest)
    panel_list = []
    for panel_index in range(neg_ids.shape[0]):
        local_rows = item_table[neg_ids[panel_index]]
        panel_list.append(broadcast(local_rows, "item", panel_owner[panel_index]))
    negatives = jnp.concatenate(panel_list, axis=0)
    loss_part, grad_rows, panel_part = loss_terms(outputs, negatives, block_mask[0], targets[0])
    panel_total, loss_total = lax.psum((panel_part, loss_part), ("seq", "item"))
    owned_panels = (panel_owner == lax.axis_index("item")).astype(jnp.float32)
    owned_rows = jnp.repeat(owned_panels, neg_ids.shape[1])
    table_grad = (
        jnp.zeros_like(item_table).at[neg_ids.reshape(-1)].add(panel_total * owned_rows[:, None])
    )
    event_total = tok_rows * lax.axis_size("seq") * lax.axis_size("item")
    return (loss_total / event_total, grad_rows[None], table_grad)


def solution(mesh):
    placed = (
        P("item", "seq", None),
        P(),
        P(),
        P(),
        P("item", None),
        P("item", None),
        P(),
        P(),
        P("item", "seq"),
        P("item", "seq"),
    )
    return jax.shard_map(
        per_device,
        mesh=mesh,
        in_specs=placed,
        out_specs=(P(), P("item", "seq", None), P("item", None)),
        check_vma=False,
    )
```

profile of v0, /device:TPU:2, one launch (start us, length us, event | category | flops | bytes accessed | tf_op | source)
XLA Modules:
  0.0 512.6 jit_solution(2004496451884381589)
XLA Ops:
  7.2 4.8 divide_multiply_fusion
  12.0 1.0 copy-done.3
  13.0 0.9 slice.60
  13.9 1.4 copy.27
  15.3 0.9 copy.28
  16.3 4.5 all-to-all-start
  21.0 0.7 fusion.57
  21.7 1.6 gather_fusion
  23.3 2.3 gather_fusion.1
  26.9 2.3 gather_fusion.2
  29.9 2.3 gather_fusion.3
  32.9 1.1 broadcast_select_fusion.3
  34.0 1.1 broadcast_select_fusion.2
  35.1 1.1 broadcast_select_fusion.1
  36.2 1.1 broadcast_select_fusion
  37.6 2.5 copy.29
  40.1 1.3 all_to_all.27
  41.4 24.4 %while.11 = (s32[]{:T(128)}, f32[2,512,2,32]{1,3,2,0:T(8,128)S(1)}, f32[1024,3,2,32]{0,3,2,1:T(8,128)S(1)}, s32[2]{0:T(128)S(1)}, s32[1024]{0:T(1024)S(1)}, /*index=5*/s32[]{:T(128)}, s32[]{:T(128)}, s32[]{:T(128)}) while((s32[]{:T(128)}, f32[2,512,2,32]{1,3,2,0:T(8,128)S(1)}, f32[1024,3,2,32]{0,3,2,1:T(8,128)S(1)}, ...), condition=%wide.region_3.4_spmd.clone, body=%wide.region_2.3_spmd.clone.sunk | while | flops 812646912 | bytes 13908123 | solution.py:83
  41.4 0.6 dynamic_slice.24
  44.0 3.6 fusion.75
  47.6 0.7 iota_add_fusion.2
  48.7 4.9 fusion.77
  53.6 0.6 dynamic_slice.24
  56.2 3.6 fusion.75
  59.8 0.7 iota_add_fusion.2
  60.9 4.9 fusion.77
  65.8 0.8 copy.35
  66.6 1.8 reshape.354
  68.3 4.6 all-to-all-start.1
  73.6 6.8 %all-to-all-done.1 = f32[8,1,8192]{2,1,0:T(1,128)S(1)} async-done(((f32[8,1,8192]{2,1,0:T(1,128)}), f32[8,1,8192]{2,1,0:T(1,128)S(1)}, u32[]{:S(2)}, u32[]{:S(2)}) %all-to-all-start.1) | async-done | bytes 262176 | tf_op jit(solution)/shard_map/all_to_all | solution.py:84
  80.9 1.3 reduce.5
  82.2 0.9 reshape.355
  83.1 1.1 copy.37
  84.2 1.0 copy.36
  85.3 1.1 copy.34
  86.3 2.1 reduce_sum.44
  88.4 1.0 fusion.37
  89.5 2.1 convolution_add_fusion
  91.6 112.1 %all-reduce.6.cloned.1.call-done = (f32[512,512]{1,0:T(8,128)}, f32[512,512]{1,0:T(8,128)}, f32[512,512]{1,0:T(8,128)}, f32[512,512]{1,0:T(8,128)}) async-done(((f32[512,512]{1,0:T(8,128)}, f32[512,512]{1,0:T(8,128)}, f32[512,512]{1,0:T(8,128)}, f32[512,512]{1,0:T(8,128)}), (f32[512,512]{1,0:T(8,128)}, f32[512,512]{1,0:T(8,128)}, f32[512,512]{1,0:T(8,128)}, ...) | async-done | bytes 4194320 | tf_op jit(solution)/shard_map/psum | solution.py:14
  203.7 1.4 constant_dynamic-update-slice_fusion.3
  205.1 1.3 constant_dynamic-update-slice_fusion.2
  206.6 2.0 copy-done.6
  208.6 6.1 %fusion.32 = (f32[]{:T(128)}, f32[128,2048]{1,0:T(8,128)S(1)}) fusion(f32[2048]{0:T(1024)S(1)} %fusion.50, s32[128]{0:T(128)S(1)} %bitcast.105, f32[128,512]{1,0:T(8,128)S(1)} %convolution_add_fusion, f32[2048,512]{1,0:T(8,128)S(1)} %constant_dynamic-update-slice_fusion), kind=kOutput, calls=%fused_computation.40 | convolution fusion | flops 1616379904 | bytes 5513732 | tf_op jit(solution)/shard_map/td,nd->tn/dot_general | solution.py:30
  214.7 5.4 %fusion.54 = f32[2048,512]{1,0:T(8,128)} fusion(f32[128,512]{1,0:T(8,128)S(1)} %convolution_add_fusion, f32[128,2048]{1,0:T(8,128)S(1)} %get-tuple-element.71, f32[2048]{0:T(1024)S(1)} %fusion.50, s32[128]{0:T(128)S(1)} %bitcast.106), kind=kOutput, calls=%fused_computation.95 | convolution fusion | flops 1614020608 | bytes 5513728 | tf_op jit(solution)/shard_map/tn,td->nd/dot_general | solution.py:45
  220.3 74.6 %psum.46 = f32[]{:T(128)} all-reduce(f32[]{:T(128)} %get-tuple-element.70), channel_id=1, replica_groups=mesh['seq'=8,'item'=32] {'seq','item'}, use_global_device_ids=true, to_apply=%region_12.13 | all-reduce | flops 1 | bytes 8 | tf_op jit(solution)/shard_map/psum | solution.py:97
  295.5 5.9 %convolution_bitcast_fusion = f32[1,128,512]{2,1,0:T(8,128)} fusion(f32[2048,512]{1,0:T(8,128)} %copy-done.6, f32[128,2048]{1,0:T(8,128)S(1)} %get-tuple-element.71, f32[2048]{0:T(1024)S(1)} %fusion.50, s32[128]{0:T(128)S(1)} %bitcast.107), kind=kOutput, calls=%fused_computation.37 | convolution fusion | flops 1614020608 | bytes 5513728 | tf_op jit(solution)/shard_map/dot_general | solution.py:44
  301.4 187.6 %all-reduce.4.cloned.1.call-done = f32[2048,512]{1,0:T(8,128)} async-done(((f32[2048,512]{1,0:T(8,128)}), f32[2048,512]{1,0:T(8,128)}) %all-reduce.4.cloned.1.call-update) | async-done | bytes 4194320 | tf_op jit(solution)/shard_map/psum | solution.py:97
  489.0 15.7 %scatter_custom_fusion = f32[1024,512]{1,0:T(8,128)} fusion(s32[2048]{0:T(1024)S(1)} %bitcast.98, f32[2048,512]{1,0:T(8,128)} %all-reduce.4.cloned.1.call-done, f32[2048]{0:T(1024)S(1)} %bitcast.95, f32[]{:T(128)} %constant.39.clone.1), kind=kCustom, calls=%fused_computation.30 | custom fusion | flops 2097152 | bytes 6299652 | tf_op jit(solution)/shard_map/scatter-add | solution.py:101
  (52 shorter events, 2.4 us)
Async XLA Ops:
  7.2 14.5 %copy-start = (f32[1024,512]{1,0:T(8,128)S(1)}, f32[1024,512]{1,0:T(8,128)}, u32[]{:S(2)}) copy-start(f32[1024,512]{1,0:T(8,128)} %param.16) | copy-start | bytes 6291460
  12.0 1.0 copy-start.3
  13.0 8.0 %copy-start.7 = (s32[4,512]{1,0:T(4,128)S(1)}, s32[4,512]{1,0:T(4,128)}, u32[]{:S(2)}) copy-start(s32[4,512]{1,0:T(4,128)} %param.18) | copy-start | bytes 24580
  13.0 8.0 %copy-start.8 = (s32[4]{0:T(128)S(1)}, s32[4]{0:T(128)}, u32[]{:S(2)}) copy-start(s32[4]{0:T(128)} %param.19) | copy-start | bytes 52
  16.3 21.4 %all-to-all-start = ((f32[128,3,16,32]{0,3,1,2:T(8,128)}), f32[128,3,16,32]{0,3,1,2:T(8,128)}, u32[]{:S(2)}, u32[]{:S(2)}) async-start(f32[128,3,16,32]{0,3,1,2:T(8,128)} %copy.28), calls=%async_computation | async-start | bytes 1572864 | tf_op jit(solution)/shard_map/all_to_all | solution.py:68
  20.7 182.9 %all-reduce.6.cloned.1.call-start = ((), (), s32[]{:S(2)}) async-start(), calls=%async_computation.3 | async-start | bytes 8388608 | tf_op jit(solution)/shard_map/psum | solution.py:14
  32.9 2.2 copy-start.1
  32.9 3.3 copy-start.2
  35.1 2.3 copy-start.10
  66.6 22.9 %copy-start.9 = (f32[512]{0:T(512)S(1)}, f32[512]{0:T(512)}, u32[]{:S(2)}) copy-start(f32[512]{0:T(512)} %param.14) | copy-start | bytes 6148
  68.3 12.1 %all-to-all-start.1 = ((f32[8,1,8192]{2,1,0:T(1,128)}), f32[8,1,8192]{2,1,0:T(1,128)S(1)}, u32[]{:S(2)}, u32[]{:S(2)}) async-start(f32[8,1,8192]{2,1,0:T(1,128)} %reshape.354), calls=%async_computation.1 | async-start | bytes 524288 | tf_op jit(solution)/shard_map/all_to_all | solution.py:84
  72.9 416.0 %all-reduce.4.cloned.1.call-start = ((), (), s32[]{:S(2)}) async-start(), calls=%async_computation.2 | async-start | bytes 8388608 | tf_op jit(solution)/shard_map/psum | solution.py:97
  203.7 2.8 copy-start.5
  203.7 2.8 copy-start.4
  203.7 4.9 copy-start.11
  206.6 2.0 copy-start.6
Sparse Core Ops, SparseCore 0:
  37.5 166.1 all-reduce.5
  220.3 268.6 all-reduce.3
where the time goes:
time: 513 us
  waiting for transfers between devices  306 us (60%)
  blocking collectives  74.6 us (15%)
  matrix products  41.3 us (8%)
  local copies, waits for them, and re-layouts  30.8 us (6%)
  other arithmetic  26.9 us (5%)
  between operations  19.3 us (4%)
  starting transfers between devices  9.29 us (2%)
    psum x1, waiting for transfers between devices, per_device(): panel_total, loss_total = lax.psum((panel_part, loss_part), ('seq', 'item'))  188 us
    psum x1, waiting for transfers between devices, broadcast(): return lax.psum(jnp.where(mine, shard, jnp.zeros_like(shard)), axis)  112 us
    psum x1, blocking collectives, per_device(): panel_total, loss_total = lax.psum((panel_part, loss_part), ('seq', 'item'))  74.6 us
    scatter-add x1, other arithmetic, per_device(): jnp.zeros_like(item_table).at[neg_ids.reshape(-1)]  15.7 us
  transfers between devices with their start and end apart: 4, of which 3 were waited for; matrix products, arithmetic and copies ran while one was open for 11% of the time, Pallas kernels for 0%

commit v1 on v0

--- a/solution.py
+++ b/solution.py
@@ -58,6 +58,12 @@
     block_mask,
     targets,
 ):
+
+    def meet_the_arrays(mesh_ax, which_axis, payload):
+        for p in (mesh_ax, which_axis):
+            payload = lax.psum(payload, p)
+        return payload
+
     rows_in = events[0]
     tok_rows, width = rows_in.shape
     head_size = width // H
@@ -94,7 +100,7 @@
         panel_list.append(broadcast(local_rows, "item", panel_owner[panel_index]))
     negatives = jnp.concatenate(panel_list, axis=0)
     loss_part, grad_rows, panel_part = loss_terms(outputs, negatives, block_mask[0], targets[0])
-    panel_total, loss_total = lax.psum((panel_part, loss_part), ("seq", "item"))
+    panel_total, loss_total = meet_the_arrays("seq", "item", (panel_part, loss_part))
     owned_panels = (panel_owner == lax.axis_index("item")).astype(jnp.float32)
     owned_rows = jnp.repeat(owned_panels, neg_ids.shape[1])
     table_grad = (

time: 513 us -> 488 us (0.951)
  waiting for transfers between devices: 306 us -> 267 us
  blocking collectives: 74.6 us -> 87.2 us
    psum x1 -> x2, waiting for transfers between devices: 188 us -> 148 us  [meet_the_arrays(): payload = lax.psum(payload, p)]
    psum x1 -> x2, blocking collectives: 74.6 us -> 87.2 us  [meet_the_arrays(): payload = lax.psum(payload, p)]
  transfers between devices with their start and end apart: 4 -> 5, of which waited for: 3 -> 4; matrix products, arithmetic and copies ran while one was open for 11% -> 12% of each run, Pallas kernels for 0% -> 0%
where the time goes in v1:
time: 488 us; the launch traced here: 486 us
  waiting for transfers between devices  267 us (55%)
  blocking collectives  87.2 us (18%)
  matrix products  41.3 us (8%)
  local copies, waits for them, and re-layouts  30.7 us (6%)
  other arithmetic  26.9 us (6%)
  between operations  19 us (4%)
  starting transfers between devices  9.34 us (2%)
    psum x2, waiting for transfers between devices, meet_the_arrays(): payload = lax.psum(payload, p)  148 us
    psum x1, waiting for transfers between devices, broadcast(): return lax.psum(jnp.where(mine, shard, jnp.zeros_like(shard)), axis)  112 us
    psum x2, blocking collectives, meet_the_arrays(): payload = lax.psum(payload, p)  87.2 us
    scatter-add x1, other arithmetic, per_device(): jnp.zeros_like(item_table).at[neg_ids.reshape(-1)]  15.7 us
  transfers between devices with their start and end apart: 5, of which 4 were waited for; matrix products, arithmetic and copies ran while one was open for 12% of the time, Pallas kernels for 0%

profile of v1, /device:TPU:2, one launch (start us, length us, event | category | flops | bytes accessed | tf_op | source)
XLA Modules:
  0.0 485.8 jit_solution(4994366870911141523)
XLA Ops:
  7.2 4.8 divide_multiply_fusion
  12.0 1.0 copy-done.3
  13.0 0.9 slice.60
  13.9 1.4 copy.27
  15.3 0.9 copy.28
  16.3 4.5 all-to-all-start
  21.0 0.7 fusion.57
  21.7 1.6 gather_fusion
  23.3 2.3 gather_fusion.1
  26.9 2.3 gather_fusion.2
  29.9 2.3 gather_fusion.3
  32.9 1.1 broadcast_select_fusion.3
  34.0 1.1 broadcast_select_fusion.2
  35.1 1.1 broadcast_select_fusion.1
  36.2 1.1 broadcast_select_fusion
  37.6 2.5 copy.29
  40.1 1.3 all_to_all.27
  41.4 24.4 %while.11 = (s32[]{:T(128)}, f32[2,512,2,32]{1,3,2,0:T(8,128)S(1)}, f32[1024,3,2,32]{0,3,2,1:T(8,128)S(1)}, s32[2]{0:T(128)S(1)}, s32[1024]{0:T(1024)S(1)}, /*index=5*/s32[]{:T(128)}, s32[]{:T(128)}, s32[]{:T(128)}) while((s32[]{:T(128)}, f32[2,512,2,32]{1,3,2,0:T(8,128)S(1)}, f32[1024,3,2,32]{0,3,2,1:T(8,128)S(1)}, ...), condition=%wide.region_3.4_spmd.clone, body=%wide.region_2.3_spmd.clone.sunk | while | flops 812646912 | bytes 13908123 | solution.py:89
  44.0 3.6 fusion.75
  47.6 0.7 iota_add_fusion.2
  48.7 4.9 %fusion.77 = f32[2,512,2,32]{1,3,2,0:T(8,128)S(1)} fusion(f32[2,512,2,32]{1,3,2,0:T(8,128)S(1)} %get-tuple-element.116, s32[]{:T(128)S(6)} %copy.44, f32[2,512,1024]{2,1,0:T(8,128)S(1)} %fusion.75, f32[512,1024]{1,0:T(8,128)S(1)} %fusion.76, f32[1024,3,2,32]{0,3,2,1:T(8,128)S(1)} %get-tuple-element.125), kind=kOutput, calls=%fused_computation.19.clone.1 | convolution fusion | flops 407896064 | bytes 6684676 | tf_op jit(solution)/shard_map/while/body/eval_jaxpr/hqk,khd->qhd/dot_general | solution.py:26
  56.2 3.6 fusion.75
  59.8 0.7 iota_add_fusion.2
  60.9 4.9 %fusion.77 = f32[2,512,2,32]{1,3,2,0:T(8,128)S(1)} fusion(f32[2,512,2,32]{1,3,2,0:T(8,128)S(1)} %get-tuple-element.116, s32[]{:T(128)S(6)} %copy.44, f32[2,512,1024]{2,1,0:T(8,128)S(1)} %fusion.75, f32[512,1024]{1,0:T(8,128)S(1)} %fusion.76, f32[1024,3,2,32]{0,3,2,1:T(8,128)S(1)} %get-tuple-element.125), kind=kOutput, calls=%fused_computation.19.clone.1 | convolution fusion | flops 407896064 | bytes 6684676 | tf_op jit(solution)/shard_map/while/body/eval_jaxpr/hqk,khd->qhd/dot_general | solution.py:26
  65.8 0.8 copy.35
  66.6 1.8 reshape.354
  68.3 4.6 all-to-all-start.1
  73.6 6.8 %all-to-all-done.1 = f32[8,1,8192]{2,1,0:T(1,128)S(1)} async-done(((f32[8,1,8192]{2,1,0:T(1,128)}), f32[8,1,8192]{2,1,0:T(1,128)S(1)}, u32[]{:S(2)}, u32[]{:S(2)}) %all-to-all-start.1) | async-done | bytes 262176 | tf_op jit(solution)/shard_map/all_to_all | solution.py:90
  80.9 1.3 reduce.5
  82.2 0.9 reshape.355
  83.1 1.1 copy.37
  84.2 1.0 copy.36
  85.3 1.1 copy.34
  86.3 2.1 reduce_sum.44
  88.4 1.0 fusion.37
  89.5 2.1 convolution_add_fusion
  91.6 112.1 %all-reduce.9.cloned.1.call-done = (f32[512,512]{1,0:T(8,128)}, f32[512,512]{1,0:T(8,128)}, f32[512,512]{1,0:T(8,128)}, f32[512,512]{1,0:T(8,128)}) async-done(((f32[512,512]{1,0:T(8,128)}, f32[512,512]{1,0:T(8,128)}, f32[512,512]{1,0:T(8,128)}, f32[512,512]{1,0:T(8,128)}), (f32[512,512]{1,0:T(8,128)}, f32[512,512]{1,0:T(8,128)}, f32[512,512]{1,0:T(8,128)}, ...) | async-done | bytes 4194320 | tf_op jit(solution)/shard_map/psum | solution.py:14
  203.7 1.4 constant_dynamic-update-slice_fusion.3
  205.1 1.3 constant_dynamic-update-slice_fusion.2
  206.6 1.9 copy-done.6
  208.5 6.1 %fusion.32 = (f32[]{:T(128)}, f32[128,2048]{1,0:T(8,128)S(1)}) fusion(f32[2048]{0:T(1024)S(1)} %fusion.50, s32[128]{0:T(128)S(1)} %bitcast.105, f32[128,512]{1,0:T(8,128)S(1)} %convolution_add_fusion, f32[2048,512]{1,0:T(8,128)S(1)} %constant_dynamic-update-slice_fusion), kind=kOutput, calls=%fused_computation.40 | convolution fusion | flops 1616379904 | bytes 5513732 | tf_op jit(solution)/shard_map/td,nd->tn/dot_general | solution.py:30
  214.6 5.4 %fusion.54 = f32[2048,512]{1,0:T(8,128)} fusion(f32[128,512]{1,0:T(8,128)S(1)} %convolution_add_fusion, f32[128,2048]{1,0:T(8,128)S(1)} %get-tuple-element.71, f32[2048]{0:T(1024)S(1)} %fusion.50, s32[128]{0:T(128)S(1)} %bitcast.106), kind=kOutput, calls=%fused_computation.95 | convolution fusion | flops 1614020608 | bytes 5513728 | tf_op jit(solution)/shard_map/tn,td->nd/dot_general | solution.py:45
  220.2 75.7 %all-reduce.5.cloned.1.call-done = f32[2048,512]{1,0:T(8,128)} async-done(((f32[2048,512]{1,0:T(8,128)}), f32[2048,512]{1,0:T(8,128)}) %all-reduce.5.cloned.1.call-update) | async-done | bytes 4194320 | tf_op jit(solution)/shard_map/psum | solution.py:64
  296.0 14.8 %psum.60 = f32[]{:T(128)} all-reduce(f32[]{:T(128)} %get-tuple-element.70), channel_id=1, replica_groups=mesh['seq'=8,'item'=32] {'seq'}, use_global_device_ids=true, to_apply=%region_12.13 | all-reduce | flops 1 | bytes 8 | tf_op jit(solution)/shard_map/psum | solution.py:64
  310.8 72.4 %psum.61 = f32[]{:T(128)} all-reduce(f32[]{:T(128)} %psum.60), channel_id=1, replica_groups=mesh['seq'=8,'item'=32] {'item'}, use_global_device_ids=true, to_apply=%region_13.14 | all-reduce | flops 1 | bytes 8 | tf_op jit(solution)/shard_map/psum | solution.py:64
  383.9 5.8 %convolution_bitcast_fusion = f32[1,128,512]{2,1,0:T(8,128)} fusion(f32[2048,512]{1,0:T(8,128)} %copy-done.6, f32[128,2048]{1,0:T(8,128)S(1)} %get-tuple-element.71, f32[2048]{0:T(1024)S(1)} %fusion.50, s32[128]{0:T(128)S(1)} %bitcast.107), kind=kOutput, calls=%fused_computation.37 | convolution fusion | flops 1614020608 | bytes 5513728 | tf_op jit(solution)/shard_map/dot_general | solution.py:44
  389.7 72.7 %all-reduce.7.cloned.1.call-done = f32[2048,512]{1,0:T(8,128)} async-done(((f32[2048,512]{1,0:T(8,128)}), f32[2048,512]{1,0:T(8,128)}) %all-reduce.7.cloned.1.call-update) | async-done | bytes 4194320 | tf_op jit(solution)/shard_map/psum | solution.py:64
  462.4 15.7 %scatter_custom_fusion = f32[1024,512]{1,0:T(8,128)} fusion(s32[2048]{0:T(1024)S(1)} %bitcast.98, f32[2048,512]{1,0:T(8,128)} %all-reduce.7.cloned.1.call-done, f32[2048]{0:T(1024)S(1)} %bitcast.95, f32[]{:T(128)} %constant.39.clone.1), kind=kCustom, calls=%fused_computation.30 | custom fusion | flops 2097152 | bytes 6299652 | tf_op jit(solution)/shard_map/scatter-add | solution.py:107
  (56 shorter events, 3.7 us)
Async XLA Ops:
  7.2 14.5 %copy-start = (f32[1024,512]{1,0:T(8,128)S(1)}, f32[1024,512]{1,0:T(8,128)}, u32[]{:S(2)}) copy-start(f32[1024,512]{1,0:T(8,128)} %param.16) | copy-start | bytes 6291460
  12.0 1.0 copy-start.3
  13.0 8.0 %copy-start.7 = (s32[4,512]{1,0:T(4,128)S(1)}, s32[4,512]{1,0:T(4,128)}, u32[]{:S(2)}) copy-start(s32[4,512]{1,0:T(4,128)} %param.18) | copy-start | bytes 24580
  13.0 8.0 %copy-start.8 = (s32[4]{0:T(128)S(1)}, s32[4]{0:T(128)}, u32[]{:S(2)}) copy-start(s32[4]{0:T(128)} %param.19) | copy-start | bytes 52
  16.3 21.4 %all-to-all-start = ((f32[128,3,16,32]{0,3,1,2:T(8,128)}), f32[128,3,16,32]{0,3,1,2:T(8,128)}, u32[]{:S(2)}, u32[]{:S(2)}) async-start(f32[128,3,16,32]{0,3,1,2:T(8,128)} %copy.28), calls=%async_computation | async-start | bytes 1572864 | tf_op jit(solution)/shard_map/all_to_all | solution.py:74
  20.7 182.9 %all-reduce.9.cloned.1.call-start = ((), (), s32[]{:S(2)}) async-start(), calls=%async_computation.4 | async-start | bytes 8388608 | tf_op jit(solution)/shard_map/psum | solution.py:14
  32.9 2.2 copy-start.1
  32.9 3.3 copy-start.2
  35.1 2.3 copy-start.10
  66.6 22.9 %copy-start.9 = (f32[512]{0:T(512)S(1)}, f32[512]{0:T(512)}, u32[]{:S(2)}) copy-start(f32[512]{0:T(512)} %param.14) | copy-start | bytes 6148
  68.3 12.1 %all-to-all-start.1 = ((f32[8,1,8192]{2,1,0:T(1,128)}), f32[8,1,8192]{2,1,0:T(1,128)S(1)}, u32[]{:S(2)}, u32[]{:S(2)}) async-start(f32[8,1,8192]{2,1,0:T(1,128)} %reshape.354), calls=%async_computation.1 | async-start | bytes 524288 | tf_op jit(solution)/shard_map/all_to_all | solution.py:90
  72.9 222.9 %all-reduce.5.cloned.1.call-start = ((), (), s32[]{:S(2)}) async-start(), calls=%async_computation.2 | async-start | bytes 8388608 | tf_op jit(solution)/shard_map/psum | solution.py:64
  203.7 2.8 copy-start.5
  203.7 2.8 copy-start.4
  203.7 4.8 copy-start.11
  206.6 1.9 copy-start.6
  220.1 242.3 %all-reduce.7.cloned.1.call-start = ((), (), s32[]{:S(2)}) async-start(), calls=%async_computation.3 | async-start | bytes 8388608 | tf_op jit(solution)/shard_map/psum | solution.py:64
Sparse Core Ops, SparseCore 0:
  37.5 166.1 all-reduce.8
  220.2 75.5 all-reduce.4
  299.4 162.9 all-reduce.6
